TPU v7x, 32 devices: a whole 2x2x4 slice. The times are simulated.
32 devices in a mesh: dp: 8 (over z, x), tensor: 4 (over y, core).
Axes of the slice: x: 2, y: 2, z: 4, core: 2. Of those that a mesh axis runs over, the one named last changes fastest.
Arguments:
- tokens: bfloat16 [20480, 768], P(('dp', 'tensor')), may hold values from -6 to 6
- lengths: int32 [8, 5], P('dp'), may hold values from 1 to 32, 40 in all within a row
- in_gain: float32 [768], replicated, may hold values from 0.25 to 1.75
- qkv_weight: bfloat16 [768, 2304], P(None, 'tensor'), may hold values from -0.21875 to 0.21875
- attn_gain: float32 [768], P('tensor'), may hold values from 0.25 to 1.75
- out_weight: bfloat16 [768, 768], P('tensor'), may hold values from -0.21875 to 0.21875
- ffn_gain: float32 [768], replicated, may hold values from 0.25 to 1.75
- up_weight: bfloat16 [768, 3072], P(None, 'tensor'), may hold values from -0.21875 to 0.21875
- hidden_gain: float32 [3072], P('tensor'), may hold values from 0.25 to 1.75
- down_weight: bfloat16 [3072, 768], P('tensor'), may hold values from -0.109375 to 0.109375
- out_grad: bfloat16 [20480, 768], P(('dp', 'tensor')), may hold values from -6 to 6
Outputs:
- output: bfloat16 [20480, 768], P(('dp', 'tensor'))
- in_grad: float32 [20480, 768], P(('dp', 'tensor'))
- grad_in_gain: float32 [768], replicated
- grad_qkv: float32 [768, 2304], P(None, 'tensor')
- grad_attn_gain: float32 [768], P('tensor')
- grad_out: float32 [768, 768], P('tensor')
- grad_ffn_gain: float32 [768], replicated
- grad_up: float32 [768, 3072], P(None, 'tensor')
- grad_hidden_gain: float32 [3072], P('tensor')
- grad_down: float32 [3072, 768], P('tensor')
Inputs may be any that keep to these rules, and one draw needn't show every extreme that they name: Each row of lengths sums to 40, and its largest entry is exactly 32.
All inputs are finite; a program needn't handle non-finite values.
Results may differ from a plain program's by a relative error of at most 0.015.
Values may be sent and summed in bfloat16 or wider, within the bound.
A program may use at most 192 MiB of HBM per device.

v0:
```python
from functools import partial
import jax
import jax.numpy as jnp
from jax import lax
from jax.sharding import PartitionSpec as P

D = 768
HEAD_DIM = 64
FF = 3072
UNIT = 64
MAXLEN = 2048
QB = 512
EPS = 1e-05


def contract_rows(left, right):
    return lax.dot_general(
        left, right, (((0,), (0,)), ((), ())), preferred_element_type=jnp.float32
    )


def contract_cols(left, right):
    return lax.dot_general(
        left, right, (((1,), (1,)), ((), ())), preferred_element_type=jnp.float32
    )


def normalize(values, gain):
    row_mean = jnp.mean(values, axis=1, keepdims=True)
    row_square = jnp.mean(values * values, axis=1, keepdims=True)
    inv_scale = lax.rsqrt(row_square - row_mean * row_mean + EPS)
    unit_rows = (values - row_mean) * inv_scale
    return (unit_rows, inv_scale, unit_rows * gain)


def norm_back(grad_normed, unit_rows, inv_scale, gain):
    weighted = grad_normed * gain
    first_mean = jnp.mean(weighted, axis=1, keepdims=True)
    second = jnp.mean(weighted * unit_rows, axis=1, keepdims=True)
    return (
        inv_scale * (weighted - first_mean - unit_rows * second),
        jnp.sum(grad_normed * unit_rows, axis=0),
    )


def segment_ids(counts, row_count):
    ends = jnp.cumsum(counts * UNIT)
    positions = jnp.arange(row_count, dtype=jnp.int32)
    return jnp.sum((positions[:, None] >= ends[None, :]).astype(jnp.int32), axis=1)


def split_heads(packed):
    row_count = packed.shape[0]
    head_count = packed.shape[1] // (3 * HEAD_DIM)
    heads_view = packed.reshape(row_count, head_count, 3, HEAD_DIM)
    return (heads_view[:, :, 0], heads_view[:, :, 1], heads_view[:, :, 2])


def block_scores(queries, keys, segment, block_index):
    row_count = queries.shape[0]
    width = MAXLEN + QB
    first_row = block_index * QB
    key_start = jnp.clip(first_row + QB - width, 0, row_count - width)
    query_block = lax.dynamic_slice_in_dim(queries, first_row, QB, 0)
    query_segment = lax.dynamic_slice_in_dim(segment, first_row, QB, 0)
    query_pos = first_row + jnp.arange(QB, dtype=jnp.int32)
    key_pos = key_start + jnp.arange(width, dtype=jnp.int32)
    allowed = (query_segment[:, None] == segment[None, :]) & (
        key_pos[None, :] <= query_pos[:, None]
    )
    score = jnp.einsum("qhe,khe->hqk", query_block, keys, preferred_element_type=jnp.float32) * (
        1.0 / float(HEAD_DIM) ** 0.5
    )
    return (jnp.where(allowed[None], score, -1000000000.0), query_block, keys, key_start)


def attention_forward(packed, segment):
    queries, keys, values = split_heads(packed)

    def one_block(block_index):
        score, query_block, key_window, key_start = block_scores(
            queries, keys, segment, block_index
        )
        top_score = jnp.max(score, axis=2, keepdims=True)
        exponent = jnp.exp(score - top_score)
        row_total = jnp.sum(exponent, axis=2, keepdims=True)
        weights = (exponent / row_total).astype(jnp.bfloat16)
        mixed = jnp.einsum("hqk,khe->qhe", weights, values, preferred_element_type=jnp.float32)
        return (mixed, (top_score + jnp.log(row_total))[:, :, 0])

    mixed, log_total = lax.map(one_block, jnp.arange(packed.shape[0] // QB, dtype=jnp.int32))
    return (mixed.reshape(packed.shape[0], -1), log_total)


def attention_backward(packed, segment, log_total, grad_mixed):
    queries, keys, values = split_heads(packed)
    row_count = packed.shape[0]
    head_count = queries.shape[1]
    grad_heads = grad_mixed.reshape(row_count, head_count, HEAD_DIM)
    scale = 1.0 / float(HEAD_DIM) ** 0.5

    def one_block(carry, block_index):
        grad_keys, grad_values = carry
        score, query_block, key_window, key_start = block_scores(
            queries, keys, segment, block_index
        )
        grad_block = lax.dynamic_slice_in_dim(grad_heads, block_index * QB, QB, 0)
        weights = jnp.exp(score - log_total[block_index][:, :, None])
        grad_weights = jnp.einsum(
            "qhe,khe->hqk", grad_block, values, preferred_element_type=jnp.float32
        )
        grad_score = (
            weights * (grad_weights - jnp.sum(weights * grad_weights, axis=2, keepdims=True))
        ).astype(jnp.bfloat16)
        grad_query = (
            jnp.einsum("hqk,khe->qhe", grad_score, key_window, preferred_element_type=jnp.float32)
            * scale
        )
        grad_key = (
            jnp.einsum("hqk,qhe->khe", grad_score, query_block, preferred_element_type=jnp.float32)
            * scale
        )
        grad_value = jnp.einsum(
            "hqk,qhe->khe",
            weights.astype(jnp.bfloat16),
            grad_block,
            preferred_element_type=jnp.float32,
        )
        grad_keys = grad_keys + grad_key
        grad_values = grad_values + grad_value
        return ((grad_keys, grad_values), grad_query)

    zeros = jnp.zeros((row_count, head_count, HEAD_DIM), jnp.float32)
    (grad_keys, grad_values), grad_queries = lax.scan(
        one_block, (zeros, zeros), jnp.arange(row_count // QB, dtype=jnp.int32)
    )
    grad_queries = grad_queries.reshape(row_count, head_count, HEAD_DIM)
    stacked = jnp.stack((grad_queries, grad_keys, grad_values), axis=2)
    return stacked.reshape(row_count, 3 * head_count * HEAD_DIM).astype(jnp.bfloat16)


def ffn_totals(grad_up, grad_down, grad_hidden):
    return lax.psum((grad_up, grad_down, grad_hidden), "dp")


def local(
    tokens,
    lengths,
    in_gain,
    qkv_weight,
    attn_gain,
    out_weight,
    ffn_gain,
    up_weight,
    hidden_gain,
    down_weight,
    out_grad,
):
    tensor_size = lax.axis_size("tensor")
    own_rows = tokens.shape[0]
    group_rows = own_rows * tensor_size
    segment = segment_ids(lengths[0], group_rows)
    residual = tokens.astype(jnp.float32)
    in_unit, in_scale, in_normed = normalize(residual, in_gain)
    gathered_in, gathered_grad = (
        lax.all_gather(in_normed.astype(jnp.bfloat16), "tensor", axis=0, tiled=True),
        lax.all_gather(out_grad, "tensor", axis=0, tiled=True),
    )
    packed = jnp.dot(gathered_in, qkv_weight, preferred_element_type=jnp.float32).astype(
        jnp.bfloat16
    )
    attended, log_total = attention_forward(packed, segment)
    att_sum, att_square = lax.psum(
        (jnp.sum(attended, axis=1), jnp.sum(attended * attended, axis=1)), "tensor"
    )
    att_mean = att_sum / D
    att_scale = lax.rsqrt(att_square / D - att_mean * att_mean + EPS)
    att_unit = (attended - att_mean[:, None]) * att_scale[:, None]
    att_low = (att_unit * attn_gain).astype(jnp.bfloat16)
    middle = residual + lax.psum_scatter(
        jnp.dot(att_low, out_weight, preferred_element_type=jnp.float32),
        "tensor",
        scatter_dimension=0,
        tiled=True,
    )
    mid_unit, mid_scale, mid_normed = normalize(middle, ffn_gain)
    mid_low = mid_normed.astype(jnp.bfloat16)
    gathered_mid = lax.all_gather(mid_low, "tensor", axis=0, tiled=True)
    pre_act = jnp.dot(gathered_mid, up_weight, preferred_element_type=jnp.float32)
    activated, gelu_pull = jax.vjp(partial(jax.nn.gelu, approximate=True), pre_act)
    act_sum, act_square = lax.psum(
        (jnp.sum(activated, axis=1), jnp.sum(activated * activated, axis=1)), "tensor"
    )
    act_mean = act_sum / FF
    act_scale = lax.rsqrt(act_square / FF - act_mean * act_mean + EPS)
    act_unit = (activated - act_mean[:, None]) * act_scale[:, None]
    act_low = (act_unit * hidden_gain).astype(jnp.bfloat16)
    result = (
        middle
        + lax.psum_scatter(
            jnp.dot(
                lax.slice_in_dim(act_low, 0, lax.axis_size("tensor") * own_rows, axis=0),
                down_weight,
                preferred_element_type=jnp.float32,
            ).astype(jnp.bfloat16),
            "tensor",
            scatter_dimension=0,
            tiled=True,
        ).astype(jnp.float32)
    ).astype(jnp.bfloat16)
    grad_down = contract_rows(act_low, gathered_grad)
    grad_act_low = contract_cols(gathered_grad, down_weight)
    weighted_act = grad_act_low * hidden_gain
    grad_hidden = jnp.sum(grad_act_low * act_unit, axis=0)
    first_sum, second_sum = lax.psum(
        (jnp.sum(weighted_act, axis=1), jnp.sum(weighted_act * act_unit, axis=1)), "tensor"
    )
    grad_act = act_scale[:, None] * (
        weighted_act - (first_sum / FF)[:, None] - act_unit * (second_sum / FF)[:, None]
    )
    grad_pre = gelu_pull(grad_act)[0].astype(jnp.bfloat16)
    grad_up = contract_rows(gathered_mid, grad_pre)
    grad_mid_normed = lax.psum_scatter(
        contract_cols(grad_pre, up_weight), "tensor", scatter_dimension=0, tiled=True
    )
    grad_mid_part, grad_ffn_gain_part = norm_back(grad_mid_normed, mid_unit, mid_scale, ffn_gain)
    grad_middle = out_grad.astype(jnp.float32) + grad_mid_part
    gathered_back = lax.all_gather(grad_middle.astype(jnp.bfloat16), "tensor", axis=0, tiled=True)
    grad_out_part = contract_rows(att_low, gathered_back)
    grad_att_low = contract_cols(gathered_back, out_weight)
    weighted_att = grad_att_low * attn_gain
    grad_attn_gain_part = jnp.sum(grad_att_low * att_unit, axis=0)
    first_att, second_att, grad_ffn_gain_group = lax.psum(
        (
            jnp.sum(weighted_att, axis=1),
            jnp.sum(weighted_att * att_unit, axis=1),
            grad_ffn_gain_part,
        ),
        "tensor",
    )
    grad_attended = (
        att_scale[:, None]
        * (weighted_att - (first_att / D)[:, None] - att_unit * (second_att / D)[:, None])
    ).astype(jnp.bfloat16)
    grad_packed = attention_backward(packed, segment, log_total, grad_attended)
    grad_qkv_part = contract_rows(gathered_in, grad_packed)
    grad_in_normed = lax.psum_scatter(
        contract_cols(grad_packed, qkv_weight).astype(jnp.bfloat16),
        "tensor",
        scatter_dimension=0,
        tiled=True,
    ).astype(jnp.float32)
    grad_in_part, grad_in_gain_part = norm_back(grad_in_normed, in_unit, in_scale, in_gain)
    in_grad = grad_middle + grad_in_part
    ffn_sums = ffn_totals(grad_up, grad_down, grad_hidden)
    attn_sums = lax.psum(
        (grad_qkv_part, grad_out_part, grad_attn_gain_part, grad_ffn_gain_group), "dp"
    )
    grad_in_gain = lax.psum(grad_in_gain_part, ("dp", "tensor"))
    return (
        result,
        in_grad,
        grad_in_gain,
        attn_sums[0],
        attn_sums[2],
        attn_sums[1],
        attn_sums[3],
        ffn_sums[0],
        ffn_sums[2],
        ffn_sums[1],
    )


def solution(mesh):
    return jax.shard_map(
        local,
        mesh=mesh,
        in_specs=(
            P(("dp", "tensor"), None),
            P("dp", None),
            P(),
            P(None, "tensor"),
            P("tensor"),
            P("tensor", None),
            P(),
            P(None, "tensor"),
            P("tensor"),
            P("tensor", None),
            P(("dp", "tensor"), None),
        ),
        out_specs=(
            P(("dp", "tensor"), None),
            P(("dp", "tensor"), None),
            P(),
            P(None, "tensor"),
            P("tensor"),
            P("tensor", None),
            P(),
            P(None, "tensor"),
            P("tensor"),
            P("tensor", None),
        ),
        check_vma=False,
    )
```

profile of v0, /device:TPU:0, one launch (start us, length us, event | category | flops | bytes accessed | tf_op | source)
XLA Modules:
  0.0 1069.0 jit_solution(10255148810879272823)
XLA Ops:
  11.9 35.5 %all-gather.5.cloned.1.call-done = bf16[2560,768]{1,0:T(8,128)(2,1)} async-done(((bf16[640,768]{1,0:T(8,128)(2,1)}), bf16[2560,768]{1,0:T(8,128)(2,1)}) %all-gather.5.cloned.1.call-update) | async-done | bytes 3932176 | tf_op jit(solution)/shard_map/all_gather | solution.py:166
  53.2 82.3 %while.37 = (s32[]{:T(128)}, f32[5,512,3,64]{1,3,2,0:T(8,128)}, f32[5,3,512]{2,1,0:T(4,128)S(1)}, s32[5]{0:T(128)S(1)}, s32[2560]{0:T(1024)S(1)}, /*index=5*/bf1...) while((s32[]{:T(128)}, f32[5,512,3,64]{1,3,2,0:T(8,128)}, ...), condition=%wide.region_7.8_spmd.clone, body=%wide.region_4.7_spmd.sunk.clone | while | flops 1057752576 | bytes 55081176 | solution.py:91
  80.7 5.4 fusion.128
  97.2 5.4 fusion.128
  113.7 5.4 fusion.128
  146.6 10.7 all-reduce.5
  157.3 6.0 fusion.52
  163.4 70.2 %reduce-scatter.5.cloned.1.call-done = f32[640,768]{1,0:T(8,128)} async-done(((f32[2560,768]{1,0:T(8,128)}), f32[640,768]{1,0:T(8,128)}) %reduce-scatter.5.cloned.1.call-update) | async-done | bytes 1966096 | tf_op jit(solution)/shard_map/reduce_scatter | solution.py:180
  238.9 32.5 %all-gather.7.cloned.1.call-done = bf16[2560,768]{1,0:T(8,128)(2,1)} async-done(((bf16[640,768]{1,0:T(8,128)(2,1)}), bf16[2560,768]{1,0:T(8,128)(2,1)}) %all-gather.7.cloned.1.call-update) | async-done | bytes 3932176 | tf_op jit(solution)/shard_map/all_gather | solution.py:188
  271.4 9.5 fusion.54
  280.9 11.6 %all-reduce.4 = (f32[2560]{0:T(1024)S(1)}, f32[2560]{0:T(1024)S(1)}) all-reduce(f32[2560]{0:T(1024)S(1)} %get-tuple-element.435, f32[2560]{0:T(1024)S(1)} %get-tuple-element.434), channel_id=1, replica_groups=mesh['dp'=8,'tensor'=4] {'tensor'}, use_global_device_ids=true, to_apply=%region_18.19 | all-reduce | flops 5120 | bytes 40960 | tf_op jit(solution)/shard_map/psum | solution.py:191
  292.6 13.9 %all-gather.9.cloned.1.call-done = bf16[2560,768]{1,0:T(8,128)(2,1)} async-done(((bf16[640,768]{1,0:T(8,128)(2,1)}), bf16[2560,768]{1,0:T(8,128)(2,1)}) %all-gather.9.cloned.1.call-update) | async-done | bytes 3932176 | tf_op jit(solution)/shard_map/all_gather | solution.py:167
  306.5 11.7 %multiply_reduce_fusion.1 = (f32[768]{0:T(1024)}, f32[2560]{0:T(1024)S(1)}, f32[2560]{0:T(1024)S(1)}, f32[2560,768]{0,1:T(8,128)}) fusion(f32[2560]{0:T(1024)S(1)} %get-tuple-element.517, f32[2560]{0:T(1024)S(1)} %get-tuple-element.516, f32[2560,768]{0,1:T(8,128)} %get-tuple-element.524, f32[768]{0:T(1024)S(1)} %copy-done.33, ...), kind=kOutput, calls=%fused_computation.52 | convolution fusion | flops 3051350272 | bytes 20887552 | tf_op jit(solution)/shard_map/dot_general | solution.py:23
  318.2 10.9 %all-reduce.3 = (f32[2560]{0:T(1024)S(1)}, f32[2560]{0:T(1024)S(1)}) all-reduce(f32[2560]{0:T(1024)S(1)} %get-tuple-element.432, f32[2560]{0:T(1024)S(1)} %get-tuple-element.433), channel_id=1, replica_groups=mesh['dp'=8,'tensor'=4] {'tensor'}, use_global_device_ids=true, to_apply=%region_23.24 | all-reduce | flops 5120 | bytes 40960 | tf_op jit(solution)/shard_map/psum | solution.py:215
  329.0 10.2 fusion.37
  341.2 5.4 fusion.58
  346.7 8.7 convolution_convert_fusion
  355.5 61.3 %reduce-scatter.9.cloned.1.call-done = f32[640,768]{1,0:T(8,128)} async-done(((f32[2560,768]{1,0:T(8,128)}), f32[640,768]{1,0:T(8,128)}) %reduce-scatter.9.cloned.1.call-update) | async-done | bytes 1966096 | tf_op jit(solution)/shard_map/reduce_scatter | solution.py:223
  419.8 42.4 %reduce-scatter.7.cloned.1.call-done = bf16[640,768]{1,0:T(8,128)(2,1)} async-done(((bf16[2560,768]{1,0:T(8,128)(2,1)}), bf16[640,768]{1,0:T(8,128)(2,1)}) %reduce-scatter.7.cloned.1.call-update) | async-done | bytes 983056 | tf_op jit(solution)/shard_map/reduce_scatter | solution.py:200
  467.5 32.0 %all-gather.11.cloned.1.call-done = bf16[2560,768]{1,0:T(8,128)(2,1)} async-done(((bf16[640,768]{1,0:T(8,128)(2,1)}), bf16[2560,768]{1,0:T(8,128)(2,1)}) %all-gather.11.cloned.1.call-update) | async-done | bytes 3932176 | tf_op jit(solution)/shard_map/all_gather | solution.py:228
  499.5 6.2 multiply_reduce_fusion.6
  505.7 11.2 %all-reduce.2 = (f32[2560]{0:T(1024)S(1)}, f32[2560]{0:T(1024)S(1)}, f32[768]{0:T(1024)}) all-reduce(f32[2560]{0:T(1024)S(1)} %get-tuple-element.437, f32[2560]{0:T(1024)S(1)} %get-tuple-element.443, f32[768]{0:T(1024)S(1)} %get-tuple-element.438), channel_id=1, replica_groups=mesh['dp'=8,'tensor'=4] {'tensor'}, use_global_device_ids=true, to_apply=%region_30.31 | all-reduce | flops 5888 | bytes 47104 | tf_op jit(solution)/shard_map/psum | solution.py:233
  519.6 234.3 %while.38 = (s32[]{:T(128)}, f32[2560,3,64]{0,2,1:T(8,128)}, f32[2560,3,64]{0,2,1:T(8,128)}, bf16[5,512,3,64]{1,3,2,0:T(8,128)(2,1)}, s32[5]{0:T(128)S(1)}, /*in...) while((s32[]{:T(128)}, f32[2560,3,64]{0,2,1:T(8,128)}, ...), condition=%wide.region_33.34_spmd.clone.clone, body=%wide.region_31.33_spmd.clone.sunk.clone | while | flops 2558461440 | bytes 171972976 | solution.py:134
  523.9 8.9 fusion.138
  532.8 9.1 multiply_reduce_fusion.15
  542.0 9.6 multiply_convert_fusion.11
  554.4 6.5 fusion.141
  568.9 9.0 fusion.138
  577.9 9.1 multiply_reduce_fusion.15
  587.0 9.6 multiply_convert_fusion.11
  600.9 6.5 fusion.141
  616.2 9.0 fusion.138
  625.2 9.1 multiply_reduce_fusion.15
  634.3 9.6 multiply_convert_fusion.11
  648.2 6.5 fusion.141
  663.5 9.0 fusion.138
  672.5 9.1 multiply_reduce_fusion.15
  681.6 9.6 multiply_convert_fusion.11
  695.5 6.5 fusion.141
  710.9 9.0 fusion.138
  719.8 9.1 multiply_reduce_fusion.15
  728.9 9.6 multiply_convert_fusion.11
  742.9 6.5 fusion.141
  769.0 8.1 fusion.59
  777.1 9.7 fusion.53
  793.4 22.6 %all-reduce = (f32[192]{0:T(256)}, f32[768]{0:T(1024)}, f32[768]{0:T(1024)}) all-reduce(f32[192]{0:T(256)S(1)} %copy-done.37, f32[768]{0:T(1024)S(1)} %copy-done.36, f32[768]{0:T(1024)S(1)} %copy-done.35), channel_id=1, replica_groups=mesh['dp'=8,'tensor'=4] {'dp'}, use_global_device_ids=true, to_apply=%region_41.42 | all-reduce | flops 1728 | bytes 13824 | tf_op jit(solution)/shard_map/psum | solution.py:256
  818.3 40.4 %psum.127 = f32[768]{0:T(1024)} all-reduce(f32[768]{0:T(1024)S(1)} %get-tuple-element.440), channel_id=1, replica_groups=mesh['dp'=8,'tensor'=4] {'dp','tensor'}, use_global_device_ids=true, to_apply=%region_38.39 | all-reduce | flops 768 | bytes 6144 | tf_op jit(solution)/shard_map/psum | solution.py:259
  862.5 193.0 %all-reduce.8.cloned.1.call-done = (f32[768,576]{0,1:T(8,128)}, f32[192,768]{1,0:T(8,128)}, f32[768,768]{1,0:T(8,128)}, f32[768,768]{1,0:T(8,128)}) async-done(((f32[768,576]{0,1:T(8,128)}, f32[192,768]{1,0:T(8,128)}, f32[768,768]{1,0:T(8,128)}, f32[768,768]{1,0:T(8,128)}), (f32[768,576]{0,1:T(8,128)}, f32[192,768]{1,0:T(8,128)}, f32[768,768]{1,0:T(8,128)}, ...) | async-done | bytes 7077904 | tf_op jit(solution)/shard_map/psum | solution.py:256
  (263 shorter events, 188.6 us)
Async XLA Ops:
  7.2 299.3 %copy-start = (bf16[768,768]{1,0:T(8,128)(2,1)S(1)}, bf16[768,768]{1,0:T(8,128)(2,1)}, u32[]{:S(2)}) copy-start(bf16[768,768]{1,0:T(8,128)(2,1)} %param.24) | copy-start | bytes 3538948
  7.2 4.4 copy-start.43
  7.2 40.2 %copy-start.41 = (bf16[768,576]{0,1:T(8,128)(2,1)S(1)}, bf16[768,576]{0,1:T(8,128)(2,1)}, u32[]{:S(2)}) copy-start(bf16[768,576]{0,1:T(8,128)(2,1)} %param.18) | copy-start | bytes 2654212
  7.2 40.2 %all-gather.5.cloned.1.call-start = ((), (), s32[]{:S(2)}) async-start(), calls=%async_computation.4 | async-start | bytes 4915200 | tf_op jit(solution)/shard_map/all_gather | solution.py:166
  9.0 43.0 %copy-start.21 = (f32[640]{0:T(1024)}, f32[640]{0:T(1024)S(1)}, u32[]{:S(2)}) copy-start(f32[640]{0:T(1024)S(1)} %get-tuple-element.522) | copy-start | bytes 7684
  9.0 43.0 %copy-start.23 = (f32[640]{0:T(1024)}, f32[640]{0:T(1024)S(1)}, u32[]{:S(2)}) copy-start(f32[640]{0:T(1024)S(1)} %get-tuple-element.523) | copy-start | bytes 7684
  11.6 222.0 %reduce-scatter.5.cloned.1.call-start = ((), (), s32[]{:S(2)}) async-start(), calls=%async_computation.5 | async-start | bytes 9830400 | tf_op jit(solution)/shard_map/reduce_scatter | solution.py:180
  137.3 20.0 %copy-start.31 = (f32[192]{0:T(256)S(1)}, f32[192]{0:T(256)}, u32[]{:S(2)}) copy-start(f32[192]{0:T(256)} %param.19) | copy-start | bytes 2308
  157.3 359.7 %copy-start.17 = (f32[2560]{0:T(1024)}, f32[2560]{0:T(1024)S(1)}, u32[]{:S(2)}) copy-start(f32[2560]{0:T(1024)S(1)} %get-tuple-element.518) | copy-start | bytes 30724
  157.3 359.7 %copy-start.19 = (f32[2560]{0:T(1024)}, f32[2560]{0:T(1024)S(1)}, u32[]{:S(2)}) copy-start(f32[2560]{0:T(1024)S(1)} %get-tuple-element.519) | copy-start | bytes 30724
  163.3 73.7 %copy-start.30 = (f32[768]{0:T(1024)S(1)}, f32[768]{0:T(1024)}, u32[]{:S(2)}) copy-start(f32[768]{0:T(1024)} %param.21) | copy-start | bytes 9220
  163.3 108.1 %all-gather.7.cloned.1.call-start = ((), (), s32[]{:S(2)}) async-start(), calls=%async_computation.6 | async-start | bytes 4915200 | tf_op jit(solution)/shard_map/all_gather | solution.py:188
  238.3 68.2 %all-gather.9.cloned.1.call-start = ((), (), s32[]{:S(2)}) async-start(), calls=%async_computation.8 | async-start | bytes 4915200 | tf_op jit(solution)/shard_map/all_gather | solution.py:167
  238.9 67.6 %copy-start.33 = (f32[768]{0:T(1024)S(1)}, f32[768]{0:T(1024)}, u32[]{:S(2)}) copy-start(f32[768]{0:T(1024)} %param.23) | copy-start | bytes 9220
  238.9 178.0 %reduce-scatter.9.cloned.1.call-start = ((), (), s32[]{:S(2)}) async-start(), calls=%async_computation.9 | async-start | bytes 9830400 | tf_op jit(solution)/shard_map/reduce_scatter | solution.py:223
  292.5 54.2 %copy-start.25 = (f32[2560]{0:T(1024)}, f32[2560]{0:T(1024)S(1)}, u32[]{:S(2)}) copy-start(f32[2560]{0:T(1024)S(1)} %get-tuple-element.516) | copy-start | bytes 30724
  292.5 54.2 %copy-start.27 = (f32[2560]{0:T(1024)}, f32[2560]{0:T(1024)S(1)}, u32[]{:S(2)}) copy-start(f32[2560]{0:T(1024)S(1)} %get-tuple-element.517) | copy-start | bytes 30724
  329.0 12.2 %copy-start.40 = (bf16[768,768]{1,0:T(8,128)(2,1)S(1)}, bf16[768,768]{1,0:T(8,128)(2,1)}, u32[]{:S(2)}) copy-start(bf16[768,768]{1,0:T(8,128)(2,1)} %param.22) | copy-start | bytes 3538948
  346.7 115.5 %reduce-scatter.7.cloned.1.call-start = ((), (), s32[]{:S(2)}) async-start(), calls=%async_computation.7 | async-start | bytes 4915200 | tf_op jit(solution)/shard_map/reduce_scatter | solution.py:200
  355.5 106.7 %copy-start.11 = (bf16[640,768]{1,0:T(8,128)(2,1)S(1)}, bf16[640,768]{1,0:T(8,128)(2,1)}, u32[]{:S(2)}) copy-start(bf16[640,768]{1,0:T(8,128)(2,1)} %param.25) | copy-start | bytes 2949124
  355.5 144.0 %all-gather.11.cloned.1.call-start = ((), (), s32[]{:S(2)}) async-start(), calls=%async_computation.10 | async-start | bytes 4915200 | tf_op jit(solution)/shard_map/all_gather | solution.py:228
  466.3 349.7 %reduce-scatter.11.cloned.1.call-start = ((), (), s32[]{:S(2)}) async-start(), calls=%async_computation.11 | async-start | bytes 4915200 | tf_op jit(solution)/shard_map/reduce_scatter | solution.py:247
  554.3 6.5 copy-start.2
  600.9 6.5 copy-start.2
  607.5 4.6 copy-start.6
  648.2 6.5 copy-start.2
  654.8 4.6 copy-start.6
  695.5 6.5 copy-start.2
  702.1 4.6 copy-start.6
  742.9 6.5 copy-start.2
  749.4 4.6 copy-start.6
  754.0 6.1 copy-start.3
  768.9 8.2 copy-start.26
  768.9 8.2 copy-start.28
  768.9 8.2 copy-start.34
  768.9 286.6 %all-reduce.8.cloned.1.call-start = ((), (), s32[]{:S(2)}) async-start(), calls=%async_computation.12 | async-start | bytes 14155776 | tf_op jit(solution)/shard_map/psum | solution.py:256
  768.9 8.1 copy-start.39
  777.1 9.8 copy-start.4
  777.1 9.8 copy-start.10
  777.1 9.8 copy-start.18
  777.1 9.8 copy-start.20
  777.1 9.8 copy-start.32
  777.1 11.6 %copy-start.38 = (bf16[2560,768]{1,0:T(8,128)(2,1)S(1)}, bf16[2560,768]{1,0:T(8,128)(2,1)}, u32[]{:S(2)}) copy-start(bf16[2560,768]{1,0:T(8,128)(2,1)} %all-gather.5.cloned.1.call-done) | copy-start | bytes 11796484
  792.7 23.3 %copy-start.8 = (bf16[640,768]{1,0:T(8,128)(2,1)S(1)}, bf16[640,768]{1,0:T(8,128)(2,1)}, u32[]{:S(2)}) copy-start(bf16[640,768]{1,0:T(8,128)(2,1)} %param.15) | copy-start | bytes 2949124
  792.7 23.3 %copy-start.22 = (f32[640]{0:T(1024)S(1)}, f32[640]{0:T(1024)}, u32[]{:S(2)}) copy-start(f32[640]{0:T(1024)} %copy-done.21) | copy-start | bytes 7684
  792.8 23.3 %copy-start.24 = (f32[640]{0:T(1024)S(1)}, f32[640]{0:T(1024)}, u32[]{:S(2)}) copy-start(f32[640]{0:T(1024)} %copy-done.23) | copy-start | bytes 7684
  792.8 23.3 %copy-start.29 = (f32[768]{0:T(1024)S(1)}, f32[768]{0:T(1024)}, u32[]{:S(2)}) copy-start(f32[768]{0:T(1024)} %param.17) | copy-start | bytes 9220
  1055.5 5.2 copy-start.14
  (17 other events, 40.5 us)
Sparse Core Ops, SparseCore 0:
  11.7 35.6 all-gather.4
  163.4 70.0 reduce-scatter.4
  238.4 32.9 all-gather.6
  272.9 33.5 all-gather.8
  346.8 70.0 reduce-scatter.8
  419.3 42.8 reduce-scatter.6
  466.4 33.0 all-gather.10
  769.0 43.9 reduce-scatter.10
  818.5 236.8 all-reduce.7
where the time goes:
time: 1080 us; the launch traced here: 1070 us
  waiting for transfers between devices  481 us (45%)
  matrix products  294 us (27%)
  other arithmetic  120 us (11%)
  blocking collectives  107 us (10%)
  local copies, waits for them, and re-layouts  36.4 us (3%)
  loops' own time  15 us (1%)
  between operations  14.9 us (1%)
    psum x1, waiting for transfers between devices, local(): lax.psum((grad_qkv_part, grad_out_part, grad_attn_gain_part, grad_ffn_gai...  193 us
    reduce_scatter x1, waiting for transfers between devices, local(): lax.psum_scatter(jnp.dot(att_low, out_weight, preferred_element_type=jnp....  70.2 us
    dot_general x10, matrix products, block_scores(): jnp.einsum('qhe,khe->hqk', query_block, keys, preferred_element_type=jnp....  66.8 us
    reduce_scatter x1, waiting for transfers between devices, local(): lax.psum_scatter(contract_cols(grad_pre, up_weight), 'tensor', scatter_di...  61.3 us
    convert_element_type x5, other arithmetic, one_block(): grad_score = (weights * (grad_weights - jnp.sum(weights * grad_weights, a...  47.9 us
    dot_general x5, matrix products, one_block(): jnp.einsum('qhe,khe->hqk', grad_block, values, preferred_element_type=jnp...  44.8 us
    reduce_scatter x1, waiting for transfers between devices, local(): lax.psum_scatter(jnp.dot(lax.slice_in_dim(act_low, 0, lax.axis_size('tens...  42.4 us
    psum x1, blocking collectives, local(): grad_in_gain = lax.psum(grad_in_gain_part, ('dp', 'tensor'))  40.4 us
  transfers between devices with their start and end apart: 9, of which 8 were waited for; matrix products, arithmetic and copies ran while one was open for 5% of the time, Pallas kernels for 0%

commit v1 on v0

--- a/solution.py
+++ b/solution.py
@@ -185,7 +185,14 @@
     )
     mid_unit, mid_scale, mid_normed = normalize(middle, ffn_gain)
     mid_low = mid_normed.astype(jnp.bfloat16)
-    gathered_mid = lax.all_gather(mid_low, "tensor", axis=0, tiled=True)
+    ring = [mid_low]
+    for hop in range(3):
+        ring.append(lax.ppermute(ring[-1], "tensor", [(dev, (dev + 1) % 4) for dev in range(4)]))
+    gathered_mid = jnp.roll(
+        jnp.concatenate(ring[::-1], axis=0),
+        (lax.axis_index("tensor") + 1) * ring[0].shape[0],
+        axis=0,
+    )
     pre_act = jnp.dot(gathered_mid, up_weight, preferred_element_type=jnp.float32)
     activated, gelu_pull = jax.vjp(partial(jax.nn.gelu, approximate=True), pre_act)
     act_sum, act_square = lax.psum(

time: 1080 us -> 1140 us (1.056)
  local copies, waits for them, and re-layouts: 36.4 us -> 70 us
  matrix products: 294 us -> 307 us
    ppermute x0 -> x3, waiting for transfers between devices: none -> 58.1 us  [local(): lax.ppermute(ring[-1], 'tensor', [(dev, (dev + 1) % 4) for dev in range(4)])]
    all_gather x1 -> x0, waiting for transfers between devices: 32.5 us -> none  [local(): gathered_mid = lax.all_gather(mid_low, 'tensor', axis=0, tiled=True)]
    while x30 -> x40, local copies, waits for them, and re-layouts: 0.06 us -> 27.6 us
    all_gather x1, waiting for transfers between devices: 13.9 us -> 0.02 us  [local(): lax.all_gather(out_grad, 'tensor', axis=0, tiled=True)]
    unnamed x87 -> x105, local copies, waits for them, and re-layouts: 17.5 us -> 23.6 us
  transfers between devices with their start and end apart: 9 -> 11, of which waited for: 8 -> 9; matrix products, arithmetic and copies ran while one was open for 5% -> 5% of each run, Pallas kernels for 0% -> 0%
where the time goes in v1:
time: 1140 us; the launch traced here: 1130 us
  waiting for transfers between devices  492 us (43%)
  matrix products  307 us (27%)
  other arithmetic  122 us (11%)
  blocking collectives  108 us (9%)
  local copies, waits for them, and re-layouts  70 us (6%)
  loops' own time  16.6 us (1%)
  between operations  15.3 us (1%)
    psum x1, waiting for transfers between devices, local(): lax.psum((grad_qkv_part, grad_out_part, grad_attn_gain_part, grad_ffn_gai...  193 us
    reduce_scatter x1, waiting for transfers between devices, local(): lax.psum_scatter(jnp.dot(att_low, out_weight, preferred_element_type=jnp....  69.4 us
    dot_general x10, matrix products, block_scores(): jnp.einsum('qhe,khe->hqk', query_block, keys, preferred_element_type=jnp....  66.8 us
    reduce_scatter x1, waiting for transfers between devices, local(): lax.psum_scatter(contract_cols(grad_pre, up_weight), 'tensor', scatter_di...  60.8 us
    ppermute x3, waiting for transfers between devices, local(): lax.ppermute(ring[-1], 'tensor', [(dev, (dev + 1) % 4) for dev in range(4)])  58.1 us
    convert_element_type x5, other arithmetic, one_block(): grad_score = (weights * (grad_weights - jnp.sum(weights * grad_weights, a...  47.7 us
    dot_general x5, matrix products, one_block(): jnp.einsum('qhe,khe->hqk', grad_block, values, preferred_element_type=jnp...  44.9 us
    reduce_scatter x1, waiting for transfers between devices, local(): lax.psum_scatter(jnp.dot(lax.slice_in_dim(act_low, 0, lax.axis_size('tens...  42.3 us
  transfers between devices with their start and end apart: 11, of which 9 were waited for; matrix products, arithmetic and copies ran while one was open for 5% of the time, Pallas kernels for 0%

profile of v1, /device:TPU:0, one launch (start us, length us, event | category | flops | bytes accessed | tf_op | source)
XLA Modules:
  0.0 1131.0 jit_solution(9551835856364223169)
XLA Ops:
  11.9 35.5 %all-gather.4.cloned.1.call-done = bf16[2560,768]{1,0:T(8,128)(2,1)} async-done(((bf16[640,768]{1,0:T(8,128)(2,1)}), bf16[2560,768]{1,0:T(8,128)(2,1)}) %all-gather.4.cloned.1.call-update) | async-done | bytes 3932176 | tf_op jit(solution)/shard_map/all_gather | solution.py:166
  53.2 82.2 %while.37 = (s32[]{:T(128)}, f32[5,512,3,64]{1,3,2,0:T(8,128)}, f32[5,3,512]{2,1,0:T(4,128)S(1)}, s32[5]{0:T(128)S(1)}, s32[2560]{0:T(1024)S(1)}, /*index=5*/bf1...) while((s32[]{:T(128)}, f32[5,512,3,64]{1,3,2,0:T(8,128)}, ...), condition=%wide.region_7.8_spmd.clone, body=%wide.region_4.7_spmd.sunk.clone | while | flops 1057752576 | bytes 55081676 | solution.py:91
  146.5 11.3 all-reduce.5
  165.3 69.4 %reduce-scatter.5.cloned.1.call-done = f32[640,768]{1,0:T(8,128)} async-done(((f32[2560,768]{1,0:T(8,128)}), f32[640,768]{1,0:T(8,128)}) %reduce-scatter.5.cloned.1.call-update) | async-done | bytes 1966096 | tf_op jit(solution)/shard_map/reduce_scatter | solution.py:180
  238.6 24.1 %collective-permute-done = bf16[640,768]{1,0:T(8,128)(2,1)S(1)} collective-permute-done((bf16[640,768]{1,0:T(8,128)(2,1)S(1)}, bf16[640,768]{1,0:T(8,128)(2,1)S(1)}, u32[]{:S(2)}, u32[]{:S(2)}) %collective-permute-start) | collective-permute-done | bytes 983072 | tf_op jit(solution)/shard_map/ppermute | solution.py:190
  263.6 20.2 %collective-permute-done.1 = bf16[640,768]{1,0:T(8,128)(2,1)} collective-permute-done((bf16[640,768]{1,0:T(8,128)(2,1)S(1)}, bf16[640,768]{1,0:T(8,128)(2,1)}, u32[]{:S(2)}, u32[]{:S(2)}) %collective-permute-start.1) | collective-permute-done | bytes 983072 | tf_op jit(solution)/shard_map/ppermute | solution.py:190
  283.8 13.8 %collective-permute-done.2 = bf16[640,768]{1,0:T(8,128)(2,1)} collective-permute-done((bf16[640,768]{1,0:T(8,128)(2,1)}, bf16[640,768]{1,0:T(8,128)(2,1)}, u32[]{:S(2)}, u32[]{:S(2)}) %collective-permute-start.2) | collective-permute-done | bytes 983072 | tf_op jit(solution)/shard_map/ppermute | solution.py:190
  303.6 7.9 fusion.60
  311.5 10.9 all-reduce.4
  323.2 11.6 %multiply_reduce_fusion.1 = (f32[768]{0:T(1024)}, f32[2560]{0:T(1024)}, f32[2560]{0:T(1024)}, f32[2560,768]{0,1:T(8,128)}) fusion(f32[2560]{0:T(1024)S(1)} %get-tuple-element.517, f32[2560]{0:T(1024)S(1)} %get-tuple-element.516, f32[2560,768]{0,1:T(8,128)} %get-tuple-element.524, f32[768]{0:T(1024)} %param.23, ...), kind=kOutput, calls=%fused_computation.52 | convolution fusion | flops 3051350272 | bytes 20887552 | tf_op jit(solution)/shard_map/dot_general | solution.py:23
  334.8 11.9 %all-reduce.3 = (f32[2560]{0:T(1024)}, f32[2560]{0:T(1024)}) all-reduce(f32[2560]{0:T(1024)} %get-tuple-element.432, f32[2560]{0:T(1024)} %get-tuple-element.433), channel_id=1, replica_groups=mesh['dp'=8,'tensor'=4] {'tensor'}, use_global_device_ids=true, to_apply=%region_23.24 | all-reduce | flops 5120 | bytes 40960 | tf_op jit(solution)/shard_map/psum | solution.py:222
  347.4 10.1 fusion.37
  364.9 8.8 convolution_convert_fusion
  373.8 60.8 %reduce-scatter.9.cloned.1.call-done = f32[640,768]{1,0:T(8,128)} async-done(((f32[2560,768]{1,0:T(8,128)}), f32[640,768]{1,0:T(8,128)}) %reduce-scatter.9.cloned.1.call-update) | async-done | bytes 1966096 | tf_op jit(solution)/shard_map/reduce_scatter | solution.py:230
  437.6 42.3 %reduce-scatter.7.cloned.1.call-done = bf16[640,768]{1,0:T(8,128)(2,1)} async-done(((bf16[2560,768]{1,0:T(8,128)(2,1)}), bf16[640,768]{1,0:T(8,128)(2,1)}) %reduce-scatter.7.cloned.1.call-update) | async-done | bytes 983056 | tf_op jit(solution)/shard_map/reduce_scatter | solution.py:207
  485.1 32.0 %all-gather.8.cloned.1.call-done = bf16[2560,768]{1,0:T(8,128)(2,1)} async-done(((bf16[640,768]{1,0:T(8,128)(2,1)}), bf16[2560,768]{1,0:T(8,128)(2,1)}) %all-gather.8.cloned.1.call-update) | async-done | bytes 3932176 | tf_op jit(solution)/shard_map/all_gather | solution.py:235
  523.2 11.3 all-reduce.2
  537.2 278.5 %while.38 = (s32[]{:T(128)}, f32[2560,3,64]{0,2,1:T(8,128)}, f32[2560,3,64]{0,2,1:T(8,128)}, bf16[5,512,3,64]{1,3,2,0:T(8,128)(2,1)}, s32[5]{0:T(128)S(1)}, /*in...) while((s32[]{:T(128)}, f32[2560,3,64]{0,2,1:T(8,128)}, ...), condition=%wide.region_33.34_spmd.clone.clone, body=%wide.region_31.33_spmd.clone.sunk.clone | while | flops 2558461440 | bytes 266345360 | solution.py:134
  539.8 9.0 fusion.141
  550.7 9.1 multiply_reduce_fusion.15
  565.4 9.5 multiply_convert_fusion.11
  574.9 6.2 fusion.142
  581.1 7.1 fusion.144
  593.7 9.0 fusion.141
  604.7 9.1 multiply_reduce_fusion.15
  619.3 9.5 multiply_convert_fusion.11
  628.9 6.8 fusion.142
  635.6 7.1 fusion.144
  649.9 9.0 fusion.141
  660.8 9.1 multiply_reduce_fusion.15
  675.4 9.5 multiply_convert_fusion.11
  685.0 6.8 fusion.142
  691.8 7.1 fusion.144
  706.0 9.0 fusion.141
  716.9 9.1 multiply_reduce_fusion.15
  731.6 9.5 multiply_convert_fusion.11
  741.1 6.8 fusion.142
  747.9 7.1 fusion.144
  762.1 9.0 fusion.141
  773.1 9.1 multiply_reduce_fusion.15
  787.7 9.5 multiply_convert_fusion.11
  797.2 6.8 fusion.142
  804.0 7.1 fusion.144
  830.6 8.1 fusion.38
  838.8 9.7 fusion.59
  855.2 22.5 %all-reduce = (f32[192]{0:T(256)}, f32[768]{0:T(1024)}, f32[768]{0:T(1024)}) all-reduce(f32[192]{0:T(256)S(1)} %copy-done.43, f32[768]{0:T(1024)S(1)} %copy-done.42, f32[768]{0:T(1024)S(1)} %copy-done.41), channel_id=1, replica_groups=mesh['dp'=8,'tensor'=4] {'dp'}, use_global_device_ids=true, to_apply=%region_41.42 | all-reduce | flops 1728 | bytes 13824 | tf_op jit(solution)/shard_map/psum | solution.py:263
  879.9 40.4 %psum.127 = f32[768]{0:T(1024)} all-reduce(f32[768]{0:T(1024)S(1)} %get-tuple-element.440), channel_id=1, replica_groups=mesh['dp'=8,'tensor'=4] {'dp','tensor'}, use_global_device_ids=true, to_apply=%region_38.39 | all-reduce | flops 768 | bytes 6144 | tf_op jit(solution)/shard_map/psum | solution.py:266
  924.1 193.0 %all-reduce.8.cloned.1.call-done = (f32[768,576]{0,1:T(8,128)}, f32[192,768]{1,0:T(8,128)}, f32[768,768]{1,0:T(8,128)}, f32[768,768]{1,0:T(8,128)}) async-done(((f32[768,576]{0,1:T(8,128)}, f32[192,768]{1,0:T(8,128)}, f32[768,768]{1,0:T(8,128)}, f32[768,768]{1,0:T(8,128)}), (f32[768,576]{0,1:T(8,128)}, f32[192,768]{1,0:T(8,128)}, f32[768,768]{1,0:T(8,128)}, ...) | async-done | bytes 7077904 | tf_op jit(solution)/shard_map/psum | solution.py:263
  (296 shorter events, 236.4 us)
Async XLA Ops:
  7.2 316.0 %copy-start = (bf16[768,768]{1,0:T(8,128)(2,1)S(1)}, bf16[768,768]{1,0:T(8,128)(2,1)}, u32[]{:S(2)}) copy-start(bf16[768,768]{1,0:T(8,128)(2,1)} %param.24) | copy-start | bytes 3538948
  7.2 40.2 %copy-start.48 = (bf16[768,576]{0,1:T(8,128)(2,1)S(1)}, bf16[768,576]{0,1:T(8,128)(2,1)}, u32[]{:S(2)}) copy-start(bf16[768,576]{0,1:T(8,128)(2,1)} %param.18) | copy-start | bytes 2654212
  7.2 40.2 %all-gather.4.cloned.1.call-start = ((), (), s32[]{:S(2)}) async-start(), calls=%async_computation.4 | async-start | bytes 4915200 | tf_op jit(solution)/shard_map/all_gather | solution.py:166
  9.0 43.0 %copy-start.28 = (f32[640]{0:T(1024)}, f32[640]{0:T(1024)S(1)}, u32[]{:S(2)}) copy-start(f32[640]{0:T(1024)S(1)} %get-tuple-element.522) | copy-start | bytes 7684
  9.0 43.0 %copy-start.30 = (f32[640]{0:T(1024)}, f32[640]{0:T(1024)S(1)}, u32[]{:S(2)}) copy-start(f32[640]{0:T(1024)S(1)} %get-tuple-element.523) | copy-start | bytes 7684
  11.6 223.2 %reduce-scatter.5.cloned.1.call-start = ((), (), s32[]{:S(2)}) async-start(), calls=%async_computation.5 | async-start | bytes 9830400 | tf_op jit(solution)/shard_map/reduce_scatter | solution.py:180
  137.2 21.3 %copy-start.21 = (bf16[192,768]{1,0:T(8,128)(2,1)S(1)}, bf16[192,768]{1,0:T(8,128)(2,1)}, u32[]{:S(2)}) copy-start(bf16[192,768]{1,0:T(8,128)(2,1)} %param.20) | copy-start | bytes 884740
  137.2 21.3 %copy-start.37 = (f32[192]{0:T(256)S(1)}, f32[192]{0:T(256)}, u32[]{:S(2)}) copy-start(f32[192]{0:T(256)} %param.19) | copy-start | bytes 2308
  158.5 376.0 %copy-start.22 = (f32[2560]{0:T(1024)}, f32[2560]{0:T(1024)S(1)}, u32[]{:S(2)}) copy-start(f32[2560]{0:T(1024)S(1)} %get-tuple-element.518) | copy-start | bytes 30724
  158.5 376.0 %copy-start.24 = (f32[2560]{0:T(1024)}, f32[2560]{0:T(1024)S(1)}, u32[]{:S(2)}) copy-start(f32[2560]{0:T(1024)S(1)} %get-tuple-element.519) | copy-start | bytes 30724
  164.5 73.7 %copy-start.27 = (f32[768]{0:T(1024)S(1)}, f32[768]{0:T(1024)}, u32[]{:S(2)}) copy-start(f32[768]{0:T(1024)} %param.21) | copy-start | bytes 9220
  164.5 158.6 %all-gather.6.cloned.1.call-start = ((), (), s32[]{:S(2)}) async-start(), calls=%async_computation.7 | async-start | bytes 4915200 | tf_op jit(solution)/shard_map/all_gather | solution.py:167
  165.3 269.3 %reduce-scatter.9.cloned.1.call-start = ((), (), s32[]{:S(2)}) async-start(), calls=%async_computation.8 | async-start | bytes 9830400 | tf_op jit(solution)/shard_map/reduce_scatter | solution.py:230
  238.5 24.2 %collective-permute-start = (bf16[640,768]{1,0:T(8,128)(2,1)S(1)}, bf16[640,768]{1,0:T(8,128)(2,1)S(1)}, u32[]{:S(2)}, u32[]{:S(2)}) collective-permute-start(bf16[640,768]{1,0:T(8,128)(2,1)S(1)} %multiply_convert_fusion.3), channel_id=1, source_target_pairs={{0,1},{1,2},{2,3},{3,0},{4,5},{5,6},{6,7},{7,4},{8,9},{9,10},{10,1... | collective-permute-start | bytes 2949128 | tf_op jit(solution)/shard_map/ppermute | solution.py:190
  263.6 20.2 %collective-permute-start.1 = (bf16[640,768]{1,0:T(8,128)(2,1)S(1)}, bf16[640,768]{1,0:T(8,128)(2,1)}, u32[]{:S(2)}, u32[]{:S(2)}) collective-permute-start(bf16[640,768]{1,0:T(8,128)(2,1)S(1)} %collective-permute-done), channel_id=1, source_target_pairs={{0,1},{1,2},{2,3},{3,0},{4,5},{5,6},{6,7},{7,4},{8,9},{9,10},{10,1... | collective-permute-start | bytes 2949128 | tf_op jit(solution)/shard_map/ppermute | solution.py:190
  283.8 13.8 %collective-permute-start.2 = (bf16[640,768]{1,0:T(8,128)(2,1)}, bf16[640,768]{1,0:T(8,128)(2,1)}, u32[]{:S(2)}, u32[]{:S(2)}) collective-permute-start(bf16[640,768]{1,0:T(8,128)(2,1)} %collective-permute-done.1), channel_id=1, source_target_pairs={{0,1},{1,2},{2,3},{3,0},{4,5},{5,6},{6,7},{7,4},{8,9},{9,10},{10,1... | collective-permute-start | bytes 2949128 | tf_op jit(solution)/shard_map/ppermute | solution.py:190
  283.8 16.4 %copy-start.15 = (bf16[640,768]{1,0:T(8,128)(2,1)S(1)}, bf16[640,768]{1,0:T(8,128)(2,1)}, u32[]{:S(2)}) copy-start(bf16[640,768]{1,0:T(8,128)(2,1)} %copy-done.14) | copy-start | bytes 2949124
  283.8 16.5 %copy-start.6 = (f32[640,768]{1,0:T(8,128)S(1)}, f32[640,768]{1,0:T(8,128)}, u32[]{:S(2)}) copy-start(f32[640,768]{1,0:T(8,128)} %copy-done.5) | copy-start | bytes 5898244
  303.6 7.9 copy-start.26
  323.1 41.8 %copy-start.32 = (f32[2560]{0:T(1024)}, f32[2560]{0:T(1024)S(1)}, u32[]{:S(2)}) copy-start(f32[2560]{0:T(1024)S(1)} %get-tuple-element.516) | copy-start | bytes 30724
  323.1 41.8 %copy-start.34 = (f32[2560]{0:T(1024)}, f32[2560]{0:T(1024)S(1)}, u32[]{:S(2)}) copy-start(f32[2560]{0:T(1024)S(1)} %get-tuple-element.517) | copy-start | bytes 30724
  347.4 12.0 %copy-start.47 = (bf16[768,768]{1,0:T(8,128)(2,1)S(1)}, bf16[768,768]{1,0:T(8,128)(2,1)}, u32[]{:S(2)}) copy-start(bf16[768,768]{1,0:T(8,128)(2,1)} %param.22) | copy-start | bytes 3538948
  364.9 115.0 %reduce-scatter.7.cloned.1.call-start = ((), (), s32[]{:S(2)}) async-start(), calls=%async_computation.6 | async-start | bytes 4915200 | tf_op jit(solution)/shard_map/reduce_scatter | solution.py:207
  373.7 106.1 %copy-start.13 = (bf16[640,768]{1,0:T(8,128)(2,1)S(1)}, bf16[640,768]{1,0:T(8,128)(2,1)}, u32[]{:S(2)}) copy-start(bf16[640,768]{1,0:T(8,128)(2,1)} %param.25) | copy-start | bytes 2949124
  373.8 143.4 %all-gather.8.cloned.1.call-start = ((), (), s32[]{:S(2)}) async-start(), calls=%async_computation.9 | async-start | bytes 4915200 | tf_op jit(solution)/shard_map/all_gather | solution.py:235
  437.6 79.6 %copy-start.38 = (f32[192]{0:T(256)S(1)}, f32[192]{0:T(256)}, u32[]{:S(2)}) copy-start(f32[192]{0:T(256)} %param.19) | copy-start | bytes 2308
  484.0 393.6 %reduce-scatter.11.cloned.1.call-start = ((), (), s32[]{:S(2)}) async-start(), calls=%async_computation.10 | async-start | bytes 4915200 | tf_op jit(solution)/shard_map/reduce_scatter | solution.py:254
  574.9 13.4 %copy-start.3 = (f32[3,512,2560]{2,1,0:T(8,128)S(1)}, f32[3,512,2560]{2,1,0:T(8,128)}, u32[]{:S(2)}) copy-start(f32[3,512,2560]{2,1,0:T(8,128)} %copy-done.2) | copy-start | bytes 47185924 | tf_op jit(solution)/shard_map/while
  628.9 13.9 %copy-start.3 = (f32[3,512,2560]{2,1,0:T(8,128)S(1)}, f32[3,512,2560]{2,1,0:T(8,128)}, u32[]{:S(2)}) copy-start(f32[3,512,2560]{2,1,0:T(8,128)} %copy-done.2) | copy-start | bytes 47185924 | tf_op jit(solution)/shard_map/while
  685.0 13.9 %copy-start.3 = (f32[3,512,2560]{2,1,0:T(8,128)S(1)}, f32[3,512,2560]{2,1,0:T(8,128)}, u32[]{:S(2)}) copy-start(f32[3,512,2560]{2,1,0:T(8,128)} %copy-done.2) | copy-start | bytes 47185924 | tf_op jit(solution)/shard_map/while
  741.1 13.9 %copy-start.3 = (f32[3,512,2560]{2,1,0:T(8,128)S(1)}, f32[3,512,2560]{2,1,0:T(8,128)}, u32[]{:S(2)}) copy-start(f32[3,512,2560]{2,1,0:T(8,128)} %copy-done.2) | copy-start | bytes 47185924 | tf_op jit(solution)/shard_map/while
  797.2 13.9 %copy-start.3 = (f32[3,512,2560]{2,1,0:T(8,128)S(1)}, f32[3,512,2560]{2,1,0:T(8,128)}, u32[]{:S(2)}) copy-start(f32[3,512,2560]{2,1,0:T(8,128)} %copy-done.2) | copy-start | bytes 47185924 | tf_op jit(solution)/shard_map/while
  815.7 7.7 copy-start.4
  830.5 8.2 copy-start.33
  830.5 8.2 copy-start.35
  830.5 8.2 copy-start.40
  830.5 286.6 %all-reduce.8.cloned.1.call-start = ((), (), s32[]{:S(2)}) async-start(), calls=%async_computation.11 | async-start | bytes 14155776 | tf_op jit(solution)/shard_map/psum | solution.py:263
  830.6 8.2 copy-start.45
  838.7 9.8 copy-start.7
  838.7 9.8 copy-start.12
  838.8 9.8 copy-start.23
  838.8 9.8 copy-start.25
  838.8 9.8 copy-start.39
  838.8 11.6 %copy-start.44 = (bf16[2560,768]{1,0:T(8,128)(2,1)S(1)}, bf16[2560,768]{1,0:T(8,128)(2,1)}, u32[]{:S(2)}) copy-start(bf16[2560,768]{1,0:T(8,128)(2,1)} %all-gather.4.cloned.1.call-done) | copy-start | bytes 11796484
  854.5 23.2 %copy-start.10 = (bf16[640,768]{1,0:T(8,128)(2,1)S(1)}, bf16[640,768]{1,0:T(8,128)(2,1)}, u32[]{:S(2)}) copy-start(bf16[640,768]{1,0:T(8,128)(2,1)} %param.15) | copy-start | bytes 2949124
  854.5 23.2 %copy-start.29 = (f32[640]{0:T(1024)S(1)}, f32[640]{0:T(1024)}, u32[]{:S(2)}) copy-start(f32[640]{0:T(1024)} %copy-done.28) | copy-start | bytes 7684
  854.5 23.2 %copy-start.31 = (f32[640]{0:T(1024)S(1)}, f32[640]{0:T(1024)}, u32[]{:S(2)}) copy-start(f32[640]{0:T(1024)} %copy-done.30) | copy-start | bytes 7684
  854.5 23.2 %copy-start.36 = (f32[768]{0:T(1024)S(1)}, f32[768]{0:T(1024)}, u32[]{:S(2)}) copy-start(f32[768]{0:T(1024)} %param.17) | copy-start | bytes 9220
  (30 other events, 89.2 us)
Sparse Core Ops, SparseCore 0:
  11.7 35.6 all-gather.3
  164.7 70.0 reduce-scatter.4
  236.4 41.6 all-gather.5
  365.0 69.5 reduce-scatter.8
  437.0 42.8 reduce-scatter.6
  484.1 32.9 all-gather.7
  830.6 43.9 reduce-scatter.10
  880.2 236.8 all-reduce.7
